TPU v7x, 32 devices: a whole 2x2x4 slice. The times are simulated.
32 devices in a mesh: dp: 16 (over z, y, core), tensor: 2 (over x).
Axes of the slice: x: 2, y: 2, z: 4, core: 2. Of those that a mesh axis runs over, the one named last changes fastest.
Arguments:
- tokens: bfloat16 [16384, 768], P(('dp', 'tensor')), may hold values from -6 to 6
- query_weight: bfloat16 [768, 768], P('dp', 'tensor'), may hold values from -0.21875 to 0.21875
- query_bias: float32 [768], replicated, may hold values from -3 to 3
- key_weight: bfloat16 [768, 768], P('dp', 'tensor'), may hold values from -0.21875 to 0.21875
- value_weight: bfloat16 [768, 768], P('dp', 'tensor'), may hold values from -0.21875 to 0.21875
- value_bias: float32 [768], replicated, may hold values from -0.625 to 0.625
- output_weight: bfloat16 [768, 768], P('tensor', 'dp'), may hold values from -1.25 to 1.25
- output_bias: float32 [768], replicated, may hold values from -3 to 3
- first_gain: float32 [768], replicated, may hold values from 0.5 to 1.5
- first_shift: float32 [768], replicated, may hold values from -3 to 3
- inner_weight: bfloat16 [768, 3072], P('dp', 'tensor'), may hold values from -0.21875 to 0.21875
- inner_bias: float32 [3072], replicated, may hold values from -3 to 3
- outer_weight: bfloat16 [3072, 768], P('tensor', 'dp'), may hold values from -0.109375 to 0.109375
- outer_bias: float32 [768], replicated, may hold values from -3 to 3
- second_gain: float32 [768], replicated, may hold values from 0.5 to 1.5
- second_shift: float32 [768], replicated, may hold values from -3 to 3
- segments: int32 [16, 1024], P('dp'), may hold values from 0 to 7, never falling along the last dimension, each value on 1 to 768 neighbouring positions
- valid_length: int32 [16], P('dp'), may hold values from 512 to 1024
- cotangent: bfloat16 [16384, 768], P(('dp', 'tensor')), may hold values from -6 to 6
Outputs:
- layer_output: bfloat16 [16384, 768], P(('dp', 'tensor'))
- input_gradient: float32 [16384, 768], P(('dp', 'tensor'))
- query_weight_gradient: float32 [768, 768], P('dp', 'tensor')
- query_bias_gradient: float32 [768], replicated
- key_weight_gradient: float32 [768, 768], P('dp', 'tensor')
- value_weight_gradient: float32 [768, 768], P('dp', 'tensor')
- value_bias_gradient: float32 [768], replicated
- output_weight_gradient: float32 [768, 768], P('tensor', 'dp')
- output_bias_gradient: float32 [768], replicated
- first_gain_gradient: float32 [768], replicated
- first_shift_gradient: float32 [768], replicated
- inner_weight_gradient: float32 [768, 3072], P('dp', 'tensor')
- inner_bias_gradient: float32 [3072], replicated
- outer_weight_gradient: float32 [3072, 768], P('tensor', 'dp')
- outer_bias_gradient: float32 [768], replicated
- second_gain_gradient: float32 [768], replicated
- second_shift_gradient: float32 [768], replicated
Inputs may be any that keep to these rules, and one draw needn't show every extreme that they name: `segments`: segment numbers never fall along a sequence; a token attends only to tokens of its own document. tokens of a sequence at positions valid_length and beyond are padding: no query attends to them as keys except the token itself.
All inputs are finite; a program needn't handle non-finite values.
Results may differ from a plain program's by a relative error of at most 0.013.
Values may be sent and summed in bfloat16 or wider, within the bound.
No kernel may reach another device: no remote copies, remote signals or barrier semaphores. Data moves between devices by JAX's collectives and lax.ppermute only.
A program may use at most 128 MiB of HBM per device.

v0:
```python
import jax
import jax.numpy as jnp
from jax import lax
from jax.sharding import PartitionSpec as P

HEAD_DIM = 64
norm_epsilon = 1e-12
masked_score = -1e30


def normalize(matrix, gain, shift):
    center = matrix - jnp.mean(matrix, axis=-1, keepdims=True)
    spread = jnp.mean(center * center, axis=-1, keepdims=True)
    return center * lax.rsqrt(spread + norm_epsilon) * gain + shift


def exact_gelu(inner):
    return jax.nn.gelu(inner, approximate=False)


def block_scores(query_block, key_seq, segment_row, valid_count, first_row):
    block_rows = query_block.shape[0]
    length = key_seq.shape[0]
    scores = (
        jnp.einsum("qhd,khd->hqk", query_block, key_seq, preferred_element_type=jnp.float32) * 0.125
    )
    positions = jnp.arange(length, dtype=jnp.int32)
    query_pos = first_row + jnp.arange(block_rows, dtype=jnp.int32)
    query_seg = lax.dynamic_slice_in_dim(segment_row, first_row, block_rows)
    allowed = (query_seg[:, None] == segment_row[None, :]) & (
        (positions[None, :] < valid_count) | (query_pos[:, None] == positions[None, :])
    )
    return jnp.where(allowed[None], scores, masked_score)


def attend_sequence(pieces):
    query_seq, key_seq, value_seq, segment_row, valid_count = pieces
    length = query_seq.shape[0]
    block_rows = min(512, length)

    def one_block(block_index):
        first_row = block_index * block_rows
        query_block = lax.dynamic_slice_in_dim(query_seq, first_row, block_rows)
        masked = block_scores(query_block, key_seq, segment_row, valid_count, first_row)
        largest = jnp.max(masked, axis=-1, keepdims=True)
        totals = jnp.sum(jnp.exp(masked - largest), axis=-1, keepdims=True)
        log_total = largest + jnp.log(totals)
        probs_low = jnp.exp(masked - log_total).astype(jnp.bfloat16)
        context = jnp.einsum(
            "hqk,khd->qhd", probs_low, value_seq, preferred_element_type=jnp.float32
        )
        return (context.astype(jnp.bfloat16), log_total[..., 0])

    contexts, log_totals = lax.map(one_block, jnp.arange(length // block_rows, dtype=jnp.int32))
    return (contexts.reshape(query_seq.shape), log_totals)


def attend_backward(pieces):
    query_seq, key_seq, value_seq, segment_row, valid_count, grad_seq, log_totals = pieces
    length = query_seq.shape[0]
    block_rows = min(512, length)

    def one_block(running, inputs):
        key_grad, value_grad = running
        block_index, log_total = inputs
        first_row = block_index * block_rows
        query_block = lax.dynamic_slice_in_dim(query_seq, first_row, block_rows)
        grad_block = lax.dynamic_slice_in_dim(grad_seq, first_row, block_rows)
        masked = block_scores(query_block, key_seq, segment_row, valid_count, first_row)
        probs = jnp.exp(masked - log_total[..., None])
        probs_low = probs.astype(jnp.bfloat16)
        value_grad = value_grad + jnp.einsum(
            "hqk,qhd->khd", probs_low, grad_block, preferred_element_type=jnp.float32
        )
        d_probs = jnp.einsum(
            "qhd,khd->hqk", grad_block, value_seq, preferred_element_type=jnp.float32
        )
        row_inner = jnp.sum(probs * d_probs, axis=-1, keepdims=True)
        d_scores = (probs * (d_probs - row_inner)).astype(jnp.bfloat16)
        query_grad = (
            jnp.einsum("hqk,khd->qhd", d_scores, key_seq, preferred_element_type=jnp.float32)
            * 0.125
        )
        key_grad = (
            key_grad
            + jnp.einsum("hqk,qhd->khd", d_scores, query_block, preferred_element_type=jnp.float32)
            * 0.125
        )
        return ((key_grad, value_grad), query_grad.astype(jnp.bfloat16))

    empty = jnp.zeros(key_seq.shape, jnp.float32)
    block_ids = jnp.arange(length // block_rows, dtype=jnp.int32)
    (key_grad, value_grad), query_grads = lax.scan(
        one_block, (empty, empty), (block_ids, log_totals)
    )
    return (
        query_grads.reshape(query_seq.shape),
        key_grad.astype(jnp.bfloat16),
        value_grad.astype(jnp.bfloat16),
    )


def place_vector(local_part, whole, shard_index):
    width = local_part.shape[0]
    return lax.dynamic_update_slice_in_dim(
        jnp.zeros((whole,), jnp.float32), local_part, shard_index * width, 0
    )


def on_device(
    tokens,
    query_weight,
    query_bias,
    key_weight,
    value_weight,
    value_bias,
    output_weight,
    output_bias,
    first_gain,
    first_shift,
    inner_weight,
    inner_bias,
    outer_weight,
    outer_bias,
    second_gain,
    second_shift,
    segments,
    valid_length,
    cotangent,
):
    head_cols = query_weight.shape[1]
    hidden_cols = inner_weight.shape[1]
    local_heads = head_cols // HEAD_DIM
    shard_index = lax.axis_index("tensor")
    bias_query = lax.dynamic_slice_in_dim(query_bias, shard_index * head_cols, head_cols)
    bias_value = lax.dynamic_slice_in_dim(value_bias, shard_index * head_cols, head_cols)
    bias_inner = lax.dynamic_slice_in_dim(inner_bias, shard_index * hidden_cols, hidden_cols)
    full_query, full_key, full_value, full_output, full_inner, full_outer = (
        lax.all_gather(query_weight, "dp", axis=0, tiled=True),
        lax.all_gather(key_weight, "dp", axis=0, tiled=True),
        lax.all_gather(value_weight, "dp", axis=0, tiled=True),
        lax.all_gather(output_weight, "dp", axis=1, tiled=True),
        lax.all_gather(inner_weight, "dp", axis=0, tiled=True),
        lax.all_gather(outer_weight, "dp", axis=1, tiled=True),
    )
    group_rows = lax.all_gather(tokens, "tensor", axis=0, tiled=True)
    seq_count = segments.shape[0]
    seq_length = segments.shape[1]
    four_shape = (seq_count, seq_length, local_heads, HEAD_DIM)
    queries = (
        jnp.dot(group_rows, full_query, preferred_element_type=jnp.float32) + bias_query
    ).astype(jnp.bfloat16)
    keys_all = jnp.dot(group_rows, full_key, preferred_element_type=jnp.float32).astype(
        jnp.bfloat16
    )
    values_all = (
        jnp.dot(group_rows, full_value, preferred_element_type=jnp.float32) + bias_value
    ).astype(jnp.bfloat16)
    queries = queries.reshape(four_shape)
    keys_all = keys_all.reshape(four_shape)
    values_all = values_all.reshape(four_shape)
    contexts, log_totals = lax.map(
        attend_sequence, (queries, keys_all, values_all, segments, valid_length)
    )
    context = contexts.reshape(seq_count * seq_length, head_cols)
    partial_attn = jnp.dot(context, full_output, preferred_element_type=jnp.float32)
    attended = lax.psum_scatter(partial_attn, "tensor", scatter_dimension=0, tiled=True)
    first_sum = tokens.astype(jnp.float32) + attended + output_bias
    hidden = normalize(first_sum, first_gain, first_shift)
    ffn_rows = lax.all_gather(hidden.astype(jnp.bfloat16), "tensor", axis=0, tiled=True)
    inner = jnp.dot(ffn_rows, full_inner, preferred_element_type=jnp.float32) + bias_inner
    activated = exact_gelu(inner).astype(jnp.bfloat16)
    partial_ffn = jnp.dot(activated, full_outer, preferred_element_type=jnp.float32)
    outer = lax.psum_scatter(partial_ffn, "tensor", scatter_dimension=0, tiled=True)
    second_sum = hidden + outer + outer_bias
    final = normalize(second_sum, second_gain, second_shift)
    layer_output = final.astype(jnp.bfloat16)
    second_value, second_pull = jax.vjp(normalize, second_sum, second_gain, second_shift)
    d_second, second_gain_grad, second_shift_grad = second_pull(cotangent.astype(jnp.float32))
    outer_bias_grad = jnp.sum(d_second, axis=0)
    d_outer = d_second.astype(jnp.bfloat16)
    held = lax.optimization_barrier(
        (query_weight, key_weight, value_weight, output_weight, inner_weight, outer_weight, d_outer)
    )
    d_outer = held[6]
    back_query, back_key, back_value, back_output, back_inner, back_outer = (
        lax.all_gather(held[0], "dp", axis=0, tiled=True),
        lax.all_gather(held[1], "dp", axis=0, tiled=True),
        lax.all_gather(held[2], "dp", axis=0, tiled=True),
        lax.all_gather(held[3], "dp", axis=1, tiled=True),
        lax.all_gather(held[4], "dp", axis=0, tiled=True),
        lax.all_gather(held[5], "dp", axis=1, tiled=True),
    )
    outer_grad_rows = lax.all_gather(d_outer, "tensor", axis=0, tiled=True)
    outer_weight_grad = jnp.einsum(
        "gf,gd->fd", activated, outer_grad_rows, preferred_element_type=jnp.float32
    )
    d_activated = jnp.einsum(
        "gd,fd->gf", outer_grad_rows, back_outer, preferred_element_type=jnp.float32
    )
    gelu_value, gelu_pull = jax.vjp(exact_gelu, inner)
    d_inner = gelu_pull(d_activated)[0].astype(jnp.bfloat16)
    inner_weight_grad = jnp.einsum(
        "gd,gf->df", ffn_rows, d_inner, preferred_element_type=jnp.float32
    )
    inner_bias_local = jnp.sum(d_inner, axis=0, dtype=jnp.float32)
    partial_hidden = jnp.einsum(
        "gf,df->gd", d_inner, back_inner, preferred_element_type=jnp.float32
    )
    d_hidden = d_second + lax.psum_scatter(
        partial_hidden, "tensor", scatter_dimension=0, tiled=True
    )
    first_value, first_pull = jax.vjp(normalize, first_sum, first_gain, first_shift)
    d_first, first_gain_grad, first_shift_grad = first_pull(d_hidden)
    output_bias_grad = jnp.sum(d_first, axis=0)
    attn_grad_rows = lax.all_gather(d_first.astype(jnp.bfloat16), "tensor", axis=0, tiled=True)
    output_weight_grad = jnp.einsum(
        "gc,gd->cd", context, attn_grad_rows, preferred_element_type=jnp.float32
    )
    d_context = jnp.einsum(
        "gd,cd->gc", attn_grad_rows, back_output, preferred_element_type=jnp.float32
    ).astype(jnp.bfloat16)
    d_queries, d_keys, d_values = lax.map(
        attend_backward,
        (
            queries,
            keys_all,
            values_all,
            segments,
            valid_length,
            d_context.reshape(four_shape),
            log_totals,
        ),
    )
    d_queries = d_queries.reshape(seq_count * seq_length, head_cols)
    d_keys = d_keys.reshape(seq_count * seq_length, head_cols)
    d_values = d_values.reshape(seq_count * seq_length, head_cols)
    query_weight_grad = jnp.einsum(
        "gd,gc->dc", group_rows, d_queries, preferred_element_type=jnp.float32
    )
    key_weight_grad = jnp.einsum(
        "gd,gc->dc", group_rows, d_keys, preferred_element_type=jnp.float32
    )
    value_weight_grad = jnp.einsum(
        "gd,gc->dc", group_rows, d_values, preferred_element_type=jnp.float32
    )
    query_bias_local = jnp.sum(d_queries, axis=0, dtype=jnp.float32)
    value_bias_local = jnp.sum(d_values, axis=0, dtype=jnp.float32)
    partial_input = jnp.einsum(
        "gc,dc->gd", d_queries, back_query, preferred_element_type=jnp.float32
    )
    partial_input = partial_input + jnp.einsum(
        "gc,dc->gd", d_keys, back_key, preferred_element_type=jnp.float32
    )
    partial_input = partial_input + jnp.einsum(
        "gc,dc->gd", d_values, back_value, preferred_element_type=jnp.float32
    )
    input_gradient = d_first + lax.psum_scatter(
        partial_input.astype(jnp.bfloat16), "tensor", scatter_dimension=0, tiled=True
    ).astype(jnp.float32)
    query_shard, key_shard, value_shard, output_shard, inner_shard, outer_shard = (
        lax.psum_scatter(query_weight_grad, "dp", scatter_dimension=0, tiled=True),
        lax.psum_scatter(key_weight_grad, "dp", scatter_dimension=0, tiled=True),
        lax.psum_scatter(value_weight_grad, "dp", scatter_dimension=0, tiled=True),
        lax.psum_scatter(output_weight_grad, "dp", scatter_dimension=1, tiled=True),
        lax.psum_scatter(inner_weight_grad, "dp", scatter_dimension=0, tiled=True),
        lax.psum_scatter(outer_weight_grad, "dp", scatter_dimension=1, tiled=True),
    )
    model_width = query_bias.shape[0]
    hidden_width = inner_bias.shape[0]
    query_bias_full = place_vector(query_bias_local, model_width, shard_index)
    value_bias_full = place_vector(value_bias_local, model_width, shard_index)
    inner_bias_full = place_vector(inner_bias_local, hidden_width, shard_index)
    summed = lax.psum(
        (
            query_bias_full,
            value_bias_full,
            output_bias_grad,
            first_gain_grad,
            first_shift_grad,
            inner_bias_full,
            outer_bias_grad,
            second_gain_grad,
            second_shift_grad,
        ),
        ("dp", "tensor"),
    )
    return (
        layer_output,
        input_gradient,
        query_shard,
        summed[0],
        key_shard,
        value_shard,
        summed[1],
        output_shard,
        summed[2],
        summed[3],
        summed[4],
        inner_shard,
        summed[5],
        outer_shard,
        summed[6],
        summed[7],
        summed[8],
    )


def solution(mesh):
    placed = (
        P(("dp", "tensor"), None),
        P("dp", "tensor"),
        P(),
        P("dp", "tensor"),
        P("dp", "tensor"),
        P(),
        P("tensor", "dp"),
        P(),
        P(),
        P(),
        P("dp", "tensor"),
        P(),
        P("tensor", "dp"),
        P(),
        P(),
        P(),
        P("dp", None),
        P("dp"),
        P(("dp", "tensor"), None),
    )
    return jax.shard_map(
        on_device,
        mesh=mesh,
        in_specs=placed,
        out_specs=(
            P(("dp", "tensor"), None),
            P(("dp", "tensor"), None),
            P("dp", "tensor"),
            P(),
            P("dp", "tensor"),
            P("dp", "tensor"),
            P(),
            P("tensor", "dp"),
            P(),
            P(),
            P(),
            P("dp", "tensor"),
            P(),
            P("tensor", "dp"),
            P(),
            P(),
            P(),
        ),
        check_vma=False,
    )
```

profile of v0, /device:TPU:0, one launch (start us, length us, event | category | flops | bytes accessed | tf_op | source)
XLA Modules:
  0.0 1077.9 jit_solution(17472114728465103642)
XLA Ops:
  10.3 25.1 %all_gather.49 = bf16[768,384]{1,0:T(8,128)(2,1)S(1)} all-gather(bf16[48,384]{1,0:T(8,128)(2,1)} %param.24), channel_id=1, replica_groups=mesh['dp'=16,'tensor'=2] {'dp'}, dimensions={0}, use_global_device_ids=true | all-gather | bytes 626688 | tf_op jit(solution)/shard_map/all_gather | solution.py:139
  54.7 20.7 %all_gather.51 = bf16[768,384]{1,0:T(8,128)(2,1)S(1)} all-gather(bf16[48,384]{1,0:T(8,128)(2,1)} %param.27), channel_id=1, replica_groups=mesh['dp'=16,'tensor'=2] {'dp'}, dimensions={0}, use_global_device_ids=true | all-gather | bytes 626688 | tf_op jit(solution)/shard_map/all_gather | solution.py:141
  75.4 20.7 %all_gather.52 = bf16[384,768]{0,1:T(8,128)(2,1)} all-gather(bf16[384,48]{0,1:T(8,128)(2,1)} %param.29), channel_id=1, replica_groups=mesh['dp'=16,'tensor'=2] {'dp'}, dimensions={1}, use_global_device_ids=true | all-gather | bytes 626688 | tf_op jit(solution)/shard_map/all_gather | solution.py:142
  100.2 34.8 %while.47 = (s32[]{:T(128)}, bf16[2,512,6,64]{1,3,2,0:T(8,128)(2,1)S(1)}, f32[2,6,512]{2,1,0:T(8,128)S(1)}, s32[2]{0:T(128)S(1)}, s32[1024]{0:T(1024)S(1)}, /*in...) while((s32[]{:T(128)}, ...), condition=%wide.region_3.4_spmd, body=%wide.region_0.3_spmd.sunk | while | flops 842201600 | bytes 92672240 | solution.py:54
  140.5 41.1 %reduce-scatter.17.cloned.1.call-done = f32[512,768]{1,0:T(8,128)} async-done(((f32[1024,768]{1,0:T(8,128)}), f32[512,768]{1,0:T(8,128)}) %reduce-scatter.17.cloned.1.call-update) | async-done | bytes 1572880 | tf_op jit(solution)/shard_map/reduce_scatter | solution.py:167
  185.7 26.4 %all-gather.11.cloned.1.call-done = bf16[1024,768]{1,0:T(8,128)(2,1)} async-done(((bf16[512,768]{1,0:T(8,128)(2,1)}), bf16[1024,768]{1,0:T(8,128)(2,1)}) %all-gather.11.cloned.1.call-update) | async-done | bytes 1572880 | tf_op jit(solution)/shard_map/all_gather | solution.py:170
  232.0 24.9 %all-gather.15.cloned.1.call-done = bf16[1536,768]{0,1:T(8,128)(2,1)} async-done(((bf16[1536,48]{0,1:T(8,128)(2,1)}), bf16[1536,768]{0,1:T(8,128)(2,1)}) %all-gather.15.cloned.1.call-update) | async-done | bytes 2359312 | tf_op jit(solution)/shard_map/all_gather | solution.py:144
  263.9 41.9 %reduce-scatter.19.cloned.1.call-done = f32[512,768]{1,0:T(8,128)} async-done(((f32[1024,768]{1,0:T(8,128)}), f32[512,768]{1,0:T(8,128)}) %reduce-scatter.19.cloned.1.call-update) | async-done | bytes 1572880 | tf_op jit(solution)/shard_map/reduce_scatter | solution.py:174
  315.8 25.2 %all-gather.17.cloned.1.call-done = bf16[1024,768]{1,0:T(8,128)(2,1)} async-done(((bf16[512,768]{1,0:T(8,128)(2,1)}), bf16[1024,768]{1,0:T(8,128)(2,1)}) %all-gather.17.cloned.1.call-update) | async-done | bytes 1572880 | tf_op jit(solution)/shard_map/all_gather | solution.py:194
  341.0 45.0 %all-gather.19.cloned.1.call-done = bf16[1536,768]{0,1:T(8,128)(2,1)} async-done(((bf16[1536,48]{0,1:T(8,128)(2,1)}), bf16[1536,768]{0,1:T(8,128)(2,1)}) %all-gather.19.cloned.1.call-update) | async-done | bytes 2359312 | tf_op jit(solution)/shard_map/all_gather | solution.py:192
  398.4 30.9 %all-gather.21.cloned.1.call-done = bf16[768,1536]{1,0:T(8,128)(2,1)} async-done(((bf16[48,1536]{1,0:T(8,128)(2,1)}), bf16[768,1536]{1,0:T(8,128)(2,1)}) %all-gather.21.cloned.1.call-update) | async-done | bytes 2359312 | tf_op jit(solution)/shard_map/all_gather | solution.py:191
  436.2 41.9 %reduce-scatter.21.cloned.1.call-done = f32[512,768]{1,0:T(8,128)} async-done(((f32[1024,768]{1,0:T(8,128)}), f32[512,768]{1,0:T(8,128)}) %reduce-scatter.21.cloned.1.call-update) | async-done | bytes 1572880 | tf_op jit(solution)/shard_map/reduce_scatter | solution.py:210
  485.0 23.1 %all_gather.60 = bf16[384,768]{0,1:T(8,128)(2,1)S(1)} all-gather(bf16[384,48]{0,1:T(8,128)(2,1)S(1)} %copy-done.23), channel_id=1, replica_groups=mesh['dp'=16,'tensor'=2] {'dp'}, dimensions={1}, use_global_device_ids=true | all-gather | bytes 626688 | tf_op jit(solution)/shard_map/all_gather | solution.py:190
  508.1 20.4 %all_gather.61 = bf16[768,384]{1,0:T(8,128)(2,1)} all-gather(bf16[48,384]{1,0:T(8,128)(2,1)S(1)} %copy-done.24), channel_id=1, replica_groups=mesh['dp'=16,'tensor'=2] {'dp'}, dimensions={0}, use_global_device_ids=true | all-gather | bytes 626688 | tf_op jit(solution)/shard_map/all_gather | solution.py:187
  528.6 22.0 %all_gather.62 = bf16[768,384]{1,0:T(8,128)(2,1)} all-gather(bf16[48,384]{1,0:T(8,128)(2,1)S(1)} %copy-done.25), channel_id=1, replica_groups=mesh['dp'=16,'tensor'=2] {'dp'}, dimensions={0}, use_global_device_ids=true | all-gather | bytes 626688 | tf_op jit(solution)/shard_map/all_gather | solution.py:188
  550.5 20.4 %all_gather.63 = bf16[768,384]{1,0:T(8,128)(2,1)} all-gather(bf16[48,384]{1,0:T(8,128)(2,1)S(1)} %copy-done.26), channel_id=1, replica_groups=mesh['dp'=16,'tensor'=2] {'dp'}, dimensions={0}, use_global_device_ids=true | all-gather | bytes 626688 | tf_op jit(solution)/shard_map/all_gather | solution.py:189
  575.1 57.7 %while.48 = (s32[]{:T(128)}, f32[1024,6,64]{0,2,1:T(8,128)S(1)}, f32[1024,6,64]{0,2,1:T(8,128)}, bf16[2,512,6,64]{1,3,2,0:T(8,128)(2,1)}, s32[2]{0:T(128)S(1)}, ...) while((s32[]{:T(128)}, f32[1024,6,64]{0,2,1:T(8,128)S(1)}, ...), condition=%wide.region_17.18_spmd.clone, body=%wide.region_15.17_spmd.clone.sunk | while | flops 2064906752 | bytes 144941456 | solution.py:93
  673.5 39.8 %all-reduce = (f32[768]{0:T(1024)}, f32[768]{0:T(1024)}, f32[768]{0:T(1024)}, f32[768]{0:T(1024)}, f32[768]{0:T(1024)}, /*index=5*/f32[3072]{0:T(1024)}, f32[768]{0:T(1024)}, f32[768]{0:T(1024)}, f32[768]{0:T(1024)}) all-reduce(f32[768]{0:T(1024)S(1)} %dynamic_update_slice.32, ...), channel_id=1, replica_groups=mesh['dp'=16,'tensor'=2] {'dp','tensor'}, use_global_device_ids=true, to_apply=%region_21.22 | all-reduce | flops 9216 | bytes 73728 | tf_op jit(solution)/shard_map/psum | solution.py:274
  715.8 29.6 %reduce-scatter.29.cloned.1.call-done = f32[1536,48]{0,1:T(8,128)} async-done(((f32[1536,768]{0,1:T(8,128)}), f32[1536,48]{0,1:T(8,128)}) %reduce-scatter.29.cloned.1.call-update) | async-done | bytes 294928 | tf_op jit(solution)/shard_map/reduce_scatter | solution.py:267
  745.5 79.0 %reduce-scatter.27.cloned.1.call-done = f32[48,1536]{1,0:T(8,128)} async-done(((f32[768,1536]{1,0:T(8,128)}), f32[48,1536]{1,0:T(8,128)}) %reduce-scatter.27.cloned.1.call-update) | async-done | bytes 294928 | tf_op jit(solution)/shard_map/reduce_scatter | solution.py:266
  824.4 61.6 %reduce-scatter.25.cloned.1.call-done = f32[384,48]{0,1:T(8,128)} async-done(((f32[384,768]{0,1:T(8,128)}), f32[384,48]{0,1:T(8,128)}) %reduce-scatter.25.cloned.1.call-update) | async-done | bytes 73744 | tf_op jit(solution)/shard_map/reduce_scatter | solution.py:265
  886.1 61.4 %reduce-scatter.35.cloned.1.call-done = f32[48,384]{1,0:T(8,128)} async-done(((f32[768,384]{1,0:T(8,128)}), f32[48,384]{1,0:T(8,128)}) %reduce-scatter.35.cloned.1.call-update) | async-done | bytes 73744
  947.4 61.5 %reduce-scatter.31.cloned.1.call-done = f32[48,384]{1,0:T(8,128)} async-done(((f32[768,384]{1,0:T(8,128)}), f32[48,384]{1,0:T(8,128)}) %reduce-scatter.31.cloned.1.call-update) | async-done | bytes 73744
  1008.9 61.2 %reduce-scatter.33.cloned.1.call-done = f32[48,384]{1,0:T(8,128)} async-done(((f32[768,384]{1,0:T(8,128)}), f32[48,384]{1,0:T(8,128)}) %reduce-scatter.33.cloned.1.call-update) | async-done | bytes 73744
  (239 shorter events, 234.1 us)
Async XLA Ops:
  8.0 88.0 %all-gather.9.cloned.1.call-start = ((), (), s32[]{:S(2)}) async-start(), calls=%async_computation.10 | async-start | bytes 2359296 | tf_op jit(solution)/shard_map/all_gather | solution.py:146
  8.8 172.9 %reduce-scatter.17.cloned.1.call-start = ((), (), s32[]{:S(2)}) async-start(), calls=%async_computation.11 | async-start | bytes 4718592 | tf_op jit(solution)/shard_map/reduce_scatter | solution.py:167
  137.0 44.7 %copy-start.13 = (bf16[512,768]{1,0:T(8,128)(2,1)S(1)}, bf16[512,768]{1,0:T(8,128)(2,1)}, u32[]{:S(2)}) copy-start(bf16[512,768]{1,0:T(8,128)(2,1)} %param.23) | copy-start | bytes 2359300
  137.0 44.7 %copy-start.36 = (f32[768]{0:T(1024)S(1)}, f32[768]{0:T(1024)}, u32[]{:S(2)}) copy-start(f32[768]{0:T(1024)} %param.30) | copy-start | bytes 9220
  139.7 46.0 %all-gather.13.cloned.1.call-start = ((), (), s32[]{:S(2)}) async-start(), calls=%async_computation.13 | async-start | bytes 2506752 | tf_op jit(solution)/shard_map/all_gather | solution.py:143
  140.3 71.8 %all-gather.11.cloned.1.call-start = ((), (), s32[]{:S(2)}) async-start(), calls=%async_computation.12 | async-start | bytes 2359296 | tf_op jit(solution)/shard_map/all_gather | solution.py:170
  185.0 72.0 %all-gather.15.cloned.1.call-start = ((), (), s32[]{:S(2)}) async-start(), calls=%async_computation.14 | async-start | bytes 2506752 | tf_op jit(solution)/shard_map/all_gather | solution.py:144
  185.5 120.2 %reduce-scatter.19.cloned.1.call-start = ((), (), s32[]{:S(2)}) async-start(), calls=%async_computation.15 | async-start | bytes 4718592 | tf_op jit(solution)/shard_map/reduce_scatter | solution.py:174
  263.8 44.3 %copy-start.12 = (bf16[512,768]{1,0:T(8,128)(2,1)S(1)}, bf16[512,768]{1,0:T(8,128)(2,1)}, u32[]{:S(2)}) copy-start(bf16[512,768]{1,0:T(8,128)(2,1)} %param.41) | copy-start | bytes 2359300
  263.9 44.3 %copy-start.30 = (f32[768]{0:T(1024)S(1)}, f32[768]{0:T(1024)}, u32[]{:S(2)}) copy-start(f32[768]{0:T(1024)} %param.37) | copy-start | bytes 9220
  263.9 77.1 %all-gather.17.cloned.1.call-start = ((), (), s32[]{:S(2)}) async-start(), calls=%async_computation.16 | async-start | bytes 2359296 | tf_op jit(solution)/shard_map/all_gather | solution.py:194
  313.8 72.1 %all-gather.19.cloned.1.call-start = ((), (), s32[]{:S(2)}) async-start(), calls=%async_computation.17 | async-start | bytes 2506752 | tf_op jit(solution)/shard_map/all_gather | solution.py:192
  314.6 114.7 %all-gather.21.cloned.1.call-start = ((), (), s32[]{:S(2)}) async-start(), calls=%async_computation.18 | async-start | bytes 2506752 | tf_op jit(solution)/shard_map/all_gather | solution.py:191
  315.3 162.8 %reduce-scatter.21.cloned.1.call-start = ((), (), s32[]{:S(2)}) async-start(), calls=%async_computation.19 | async-start | bytes 4718592 | tf_op jit(solution)/shard_map/reduce_scatter | solution.py:210
  436.2 134.8 %all-gather.23.cloned.1.call-start = ((), (), s32[]{:S(2)}) async-start(), calls=%async_computation.20 | async-start | bytes 2359296 | tf_op jit(solution)/shard_map/all_gather | solution.py:216
  482.1 46.5 %copy-start.25 = (bf16[48,384]{1,0:T(8,128)(2,1)S(1)}, bf16[48,384]{1,0:T(8,128)(2,1)}, u32[]{:S(2)}) copy-start(bf16[48,384]{1,0:T(8,128)(2,1)} %param.26) | copy-start | bytes 110596
  482.1 68.4 %copy-start.26 = (bf16[48,384]{1,0:T(8,128)(2,1)S(1)}, bf16[48,384]{1,0:T(8,128)(2,1)}, u32[]{:S(2)}) copy-start(bf16[48,384]{1,0:T(8,128)(2,1)} %param.27) | copy-start | bytes 110596
  484.9 228.4 %reduce-scatter.23.cloned.1.call-start = ((), (), s32[]{:S(2)}) async-start(), calls=%async_computation.21 | async-start | bytes 2359296 | tf_op jit(solution)/shard_map/reduce_scatter | solution.py:258
  641.2 104.2 %reduce-scatter.29.cloned.1.call-start = ((), (), s32[]{:S(2)}) async-start(), calls=%async_computation.24 | async-start | bytes 5013504 | tf_op jit(solution)/shard_map/reduce_scatter | solution.py:267
  648.4 176.0 %reduce-scatter.27.cloned.1.call-start = ((), (), s32[]{:S(2)}) async-start(), calls=%async_computation.23 | async-start | bytes 5013504 | tf_op jit(solution)/shard_map/reduce_scatter | solution.py:266
  655.7 230.4 %reduce-scatter.25.cloned.1.call-start = ((), (), s32[]{:S(2)}) async-start(), calls=%async_computation.22 | async-start | bytes 1253376 | tf_op jit(solution)/shard_map/reduce_scatter | solution.py:265
  660.4 287.1 %reduce-scatter.35.cloned.1.call-start = ((), (), s32[]{:S(2)}) async-start(), calls=%async_computation.27 | async-start | bytes 1253376
  664.1 344.8 %reduce-scatter.31.cloned.1.call-start = ((), (), s32[]{:S(2)}) async-start(), calls=%async_computation.25 | async-start | bytes 1253376
  667.8 402.3 %reduce-scatter.33.cloned.1.call-start = ((), (), s32[]{:S(2)}) async-start(), calls=%async_computation.26 | async-start | bytes 1253376
  (39 other events, 351.9 us)
Sparse Core Ops, SparseCore 0:
  10.4 29.8 all-gather.8
  139.8 41.8 reduce-scatter.16
  264.0 41.7 reduce-scatter.18
  436.3 41.7 reduce-scatter.20
  485.0 27.1 all-gather.22
Sparse Core Ops, SparseCore 1:
  142.5 40.8 all-gather.12
  185.3 26.7 all-gather.10
  214.3 42.6 all-gather.14
  313.9 27.0 all-gather.16
  343.3 42.6 all-gather.18
  388.2 40.9 all-gather.20
  641.3 23.6 reduce-scatter.22
  669.3 76.1 reduce-scatter.28
  749.8 74.6 reduce-scatter.26
  828.7 57.3 reduce-scatter.24
  890.1 57.2 reduce-scatter.34
  951.6 57.2 reduce-scatter.30
  1013.0 57.1 reduce-scatter.32
where the time goes:
time: 1090 us; the launch traced here: 1080 us
  waiting for transfers between devices  635 us (58%)
  blocking collectives  212 us (19%)
  matrix products  147 us (13%)
  other arithmetic  42.9 us (4%)
  local copies, waits for them, and re-layouts  20.5 us (2%)
  between operations  16.7 us (2%)
    unnamed x21, waiting for transfers between devices  187 us
    reduce_scatter x1, waiting for transfers between devices, on_device(): lax.psum_scatter(inner_weight_grad, 'dp', scatter_dimension=0, tiled=True)  79 us
    reduce_scatter x1, waiting for transfers between devices, on_device(): lax.psum_scatter(output_weight_grad, 'dp', scatter_dimension=1, tiled=True)  61.6 us
    all_gather x1, waiting for transfers between devices, on_device(): lax.all_gather(held[5], 'dp', axis=1, tiled=True)  45 us
    reduce_scatter x1, waiting for transfers between devices, on_device(): lax.psum_scatter(partial_hidden, 'tensor', scatter_dimension=0, tiled=True)  41.9 us
    reduce_scatter x1, waiting for transfers between devices, on_device(): lax.psum_scatter(partial_ffn, 'tensor', scatter_dimension=0, tiled=True)  41.9 us
    reduce_scatter x1, waiting for transfers between devices, on_device(): lax.psum_scatter(partial_attn, 'tensor', scatter_dimension=0, tiled=True)  41.1 us
    psum x1, blocking collectives, on_device(): lax.psum((query_bias_full, value_bias_full, output_bias_grad, first_gain_...  39.8 us
  transfers between devices with their start and end apart: 18, of which 14 were waited for; matrix products, arithmetic and copies ran while one was open for 6% of the time, Pallas kernels for 0%

commit v1 on v0

--- a/solution.py
+++ b/solution.py
@@ -1,3 +1,4 @@
+import functools
 import jax
 import jax.numpy as jnp
 from jax import lax
@@ -6,6 +7,34 @@
 HEAD_DIM = 64
 norm_epsilon = 1e-12
 masked_score = -1e30
+
+
+def _write_edges(u_in, ndim_at):
+    carry_out = list(u_in.shape[1:])
+    carry_out[ndim_at] *= u_in.shape[0]
+    return jnp.moveaxis(u_in, 0, ndim_at).reshape(carry_out)
+
+
+def launch_rings_here(target, link_axis):
+    raw_out = target[None]
+    degree = lax.axis_size(link_axis)
+    for dev in range(degree.bit_length() - 1):
+        v_next = 1 << dev
+        queue = []
+        for dev_j in range(degree):
+            queue.append((dev_j, dev_j ^ v_next))
+        view_out = lax.ppermute(raw_out, link_axis, queue)
+        item_now = jnp.stack([raw_out, view_out])
+        answer = lax.axis_index(link_axis) >> dev & 1
+        raw_out = jnp.where(answer == 0, item_now, item_now[::-1]).reshape(-1, *target.shape)
+    return raw_out
+
+
+def create_yards_over_axis(arr, view, in_dim):
+    return _write_edges(launch_rings_here(arr, view), in_dim)
+
+
+_try_all_cells = functools.partial(create_yards_over_axis, view="dp", in_dim=0)
 
 
 def normalize(matrix, gain, shift):
@@ -136,7 +165,7 @@
     bias_value = lax.dynamic_slice_in_dim(value_bias, shard_index * head_cols, head_cols)
     bias_inner = lax.dynamic_slice_in_dim(inner_bias, shard_index * hidden_cols, hidden_cols)
     full_query, full_key, full_value, full_output, full_inner, full_outer = (
-        lax.all_gather(query_weight, "dp", axis=0, tiled=True),
+        _try_all_cells(query_weight),
         lax.all_gather(key_weight, "dp", axis=0, tiled=True),
         lax.all_gather(value_weight, "dp", axis=0, tiled=True),
         lax.all_gather(output_weight, "dp", axis=1, tiled=True),

time: 1090 us -> 1080 us (level)
  blocking collectives: 212 us -> 195 us
    all_gather x1 -> x0, blocking collectives: 25.1 us -> none  [on_device(): lax.all_gather(query_weight, 'dp', axis=0, tiled=True)]
  transfers between devices with their start and end apart: 18 -> 22, of which waited for: 14 -> 16; matrix products, arithmetic and copies ran while one was open for 6% -> 6% of each run, Pallas kernels for 0% -> 0%
where the time goes in v1:
time: 1080 us; the launch traced here: 1070 us
  waiting for transfers between devices  637 us (59%)
  blocking collectives  195 us (18%)
  matrix products  146 us (14%)
  other arithmetic  44 us (4%)
  local copies, waits for them, and re-layouts  19.2 us (2%)
  between operations  16.8 us (2%)
    unnamed x21, waiting for transfers between devices  187 us
    reduce_scatter x1, waiting for transfers between devices, on_device(): lax.psum_scatter(inner_weight_grad, 'dp', scatter_dimension=0, tiled=True)  79.1 us
    reduce_scatter x1, waiting for transfers between devices, on_device(): lax.psum_scatter(output_weight_grad, 'dp', scatter_dimension=1, tiled=True)  61.7 us
    all_gather x1, waiting for transfers between devices, on_device(): lax.all_gather(held[5], 'dp', axis=1, tiled=True)  45 us
    reduce_scatter x1, waiting for transfers between devices, on_device(): lax.psum_scatter(partial_hidden, 'tensor', scatter_dimension=0, tiled=True)  41.9 us
    reduce_scatter x1, waiting for transfers between devices, on_device(): lax.psum_scatter(partial_ffn, 'tensor', scatter_dimension=0, tiled=True)  41.9 us
    reduce_scatter x1, waiting for transfers between devices, on_device(): lax.psum_scatter(partial_attn, 'tensor', scatter_dimension=0, tiled=True)  40.2 us
    psum x1, blocking collectives, on_device(): lax.psum((query_bias_full, value_bias_full, output_bias_grad, first_gain_...  39.8 us
  transfers between devices with their start and end apart: 22, of which 16 were waited for; matrix products, arithmetic and copies ran while one was open for 6% of the time, Pallas kernels for 0%

profile of v1, /device:TPU:0, one launch (start us, length us, event | category | flops | bytes accessed | tf_op | source)
XLA Modules:
  0.0 1068.7 jit_solution(13991400669540701747)
XLA Ops:
  18.0 22.4 %all_gather.46 = bf16[768,384]{1,0:T(8,128)(2,1)S(1)} all-gather(bf16[48,384]{1,0:T(8,128)(2,1)} %param.26), channel_id=1, replica_groups=mesh['dp'=16,'tensor'=2] {'dp'}, dimensions={0}, use_global_device_ids=true | all-gather | bytes 626688 | tf_op jit(solution)/shard_map/all_gather | solution.py:169
  40.6 24.9 %all_gather.47 = bf16[768,384]{1,0:T(8,128)(2,1)S(1)} all-gather(bf16[48,384]{1,0:T(8,128)(2,1)S(1)} %copy-done.26), channel_id=1, replica_groups=mesh['dp'=16,'tensor'=2] {'dp'}, dimensions={0}, use_global_device_ids=true | all-gather | bytes 626688 | tf_op jit(solution)/shard_map/all_gather | solution.py:170
  65.6 22.1 %all_gather.48 = bf16[384,768]{0,1:T(8,128)(2,1)} all-gather(bf16[384,48]{0,1:T(8,128)(2,1)S(1)} %copy-done.23), channel_id=1, replica_groups=mesh['dp'=16,'tensor'=2] {'dp'}, dimensions={1}, use_global_device_ids=true | all-gather | bytes 626688 | tf_op jit(solution)/shard_map/all_gather | solution.py:171
  92.0 34.8 %while.47 = (s32[]{:T(128)}, bf16[2,512,6,64]{1,3,2,0:T(8,128)(2,1)S(1)}, f32[2,6,512]{2,1,0:T(8,128)S(1)}, s32[2]{0:T(128)S(1)}, s32[1024]{0:T(1024)S(1)}, /*in...) while((s32[]{:T(128)}, ...), condition=%wide.region_3.4_spmd, body=%wide.region_0.3_spmd.sunk | while | flops 842201600 | bytes 92672240 | solution.py:83
  132.1 40.2 %reduce-scatter.17.cloned.1.call-done = f32[512,768]{1,0:T(8,128)} async-done(((f32[1024,768]{1,0:T(8,128)}), f32[512,768]{1,0:T(8,128)}) %reduce-scatter.17.cloned.1.call-update) | async-done | bytes 1572880 | tf_op jit(solution)/shard_map/reduce_scatter | solution.py:196
  176.3 26.4 %all-gather.11.cloned.1.call-done = bf16[1024,768]{1,0:T(8,128)(2,1)} async-done(((bf16[512,768]{1,0:T(8,128)(2,1)}), bf16[1024,768]{1,0:T(8,128)(2,1)}) %all-gather.11.cloned.1.call-update) | async-done | bytes 1572880 | tf_op jit(solution)/shard_map/all_gather | solution.py:199
  222.6 24.8 %all-gather.15.cloned.1.call-done = bf16[1536,768]{0,1:T(8,128)(2,1)} async-done(((bf16[1536,48]{0,1:T(8,128)(2,1)}), bf16[1536,768]{0,1:T(8,128)(2,1)}) %all-gather.15.cloned.1.call-update) | async-done | bytes 2359312 | tf_op jit(solution)/shard_map/all_gather | solution.py:173
  254.4 41.9 %reduce-scatter.19.cloned.1.call-done = f32[512,768]{1,0:T(8,128)} async-done(((f32[1024,768]{1,0:T(8,128)}), f32[512,768]{1,0:T(8,128)}) %reduce-scatter.19.cloned.1.call-update) | async-done | bytes 1572880 | tf_op jit(solution)/shard_map/reduce_scatter | solution.py:203
  306.2 25.2 %all-gather.17.cloned.1.call-done = bf16[1024,768]{1,0:T(8,128)(2,1)} async-done(((bf16[512,768]{1,0:T(8,128)(2,1)}), bf16[1024,768]{1,0:T(8,128)(2,1)}) %all-gather.17.cloned.1.call-update) | async-done | bytes 1572880 | tf_op jit(solution)/shard_map/all_gather | solution.py:223
  331.5 45.0 %all-gather.19.cloned.1.call-done = bf16[1536,768]{0,1:T(8,128)(2,1)} async-done(((bf16[1536,48]{0,1:T(8,128)(2,1)}), bf16[1536,768]{0,1:T(8,128)(2,1)}) %all-gather.19.cloned.1.call-update) | async-done | bytes 2359312 | tf_op jit(solution)/shard_map/all_gather | solution.py:221
  388.8 30.9 %all-gather.21.cloned.1.call-done = bf16[768,1536]{1,0:T(8,128)(2,1)} async-done(((bf16[48,1536]{1,0:T(8,128)(2,1)}), bf16[768,1536]{1,0:T(8,128)(2,1)}) %all-gather.21.cloned.1.call-update) | async-done | bytes 2359312 | tf_op jit(solution)/shard_map/all_gather | solution.py:220
  426.7 41.9 %reduce-scatter.21.cloned.1.call-done = f32[512,768]{1,0:T(8,128)} async-done(((f32[1024,768]{1,0:T(8,128)}), f32[512,768]{1,0:T(8,128)}) %reduce-scatter.21.cloned.1.call-update) | async-done | bytes 1572880 | tf_op jit(solution)/shard_map/reduce_scatter | solution.py:239
  475.5 23.1 %all_gather.56 = bf16[384,768]{0,1:T(8,128)(2,1)S(1)} all-gather(bf16[384,48]{0,1:T(8,128)(2,1)S(1)} %copy-done.24), channel_id=1, replica_groups=mesh['dp'=16,'tensor'=2] {'dp'}, dimensions={1}, use_global_device_ids=true | all-gather | bytes 626688 | tf_op jit(solution)/shard_map/all_gather | solution.py:219
  498.6 20.4 %all_gather.57 = bf16[768,384]{1,0:T(8,128)(2,1)} all-gather(bf16[48,384]{1,0:T(8,128)(2,1)S(1)} %copy-done.28), channel_id=1, replica_groups=mesh['dp'=16,'tensor'=2] {'dp'}, dimensions={0}, use_global_device_ids=true | all-gather | bytes 626688 | tf_op jit(solution)/shard_map/all_gather | solution.py:216
  519.1 22.0 %all_gather.58 = bf16[768,384]{1,0:T(8,128)(2,1)} all-gather(bf16[48,384]{1,0:T(8,128)(2,1)S(1)} %copy-done.25), channel_id=1, replica_groups=mesh['dp'=16,'tensor'=2] {'dp'}, dimensions={0}, use_global_device_ids=true | all-gather | bytes 626688 | tf_op jit(solution)/shard_map/all_gather | solution.py:217
  541.0 20.4 %all_gather.59 = bf16[768,384]{1,0:T(8,128)(2,1)} all-gather(bf16[48,384]{1,0:T(8,128)(2,1)S(1)} %copy-done.27), channel_id=1, replica_groups=mesh['dp'=16,'tensor'=2] {'dp'}, dimensions={0}, use_global_device_ids=true | all-gather | bytes 626688 | tf_op jit(solution)/shard_map/all_gather | solution.py:218
  565.5 57.7 %while.48 = (s32[]{:T(128)}, f32[1024,6,64]{0,2,1:T(8,128)S(1)}, f32[1024,6,64]{0,2,1:T(8,128)}, bf16[2,512,6,64]{1,3,2,0:T(8,128)(2,1)}, s32[2]{0:T(128)S(1)}, ...) while((s32[]{:T(128)}, f32[1024,6,64]{0,2,1:T(8,128)S(1)}, ...), condition=%wide.region_17.18_spmd.clone, body=%wide.region_15.17_spmd.clone.sunk | while | flops 2064906752 | bytes 144941456 | solution.py:122
  664.0 39.8 %all-reduce = (f32[768]{0:T(1024)}, f32[768]{0:T(1024)}, f32[768]{0:T(1024)}, f32[768]{0:T(1024)}, f32[768]{0:T(1024)}, /*index=5*/f32[3072]{0:T(1024)}, f32[768]{0:T(1024)}, f32[768]{0:T(1024)}, f32[768]{0:T(1024)}) all-reduce(f32[768]{0:T(1024)S(1)} %dynamic_update_slice.32, ...), channel_id=1, replica_groups=mesh['dp'=16,'tensor'=2] {'dp','tensor'}, use_global_device_ids=true, to_apply=%region_21.22 | all-reduce | flops 9216 | bytes 73728 | tf_op jit(solution)/shard_map/psum | solution.py:303
  706.3 29.6 %reduce-scatter.29.cloned.1.call-done = f32[1536,48]{0,1:T(8,128)} async-done(((f32[1536,768]{0,1:T(8,128)}), f32[1536,48]{0,1:T(8,128)}) %reduce-scatter.29.cloned.1.call-update) | async-done | bytes 294928 | tf_op jit(solution)/shard_map/reduce_scatter | solution.py:296
  736.0 79.1 %reduce-scatter.27.cloned.1.call-done = f32[48,1536]{1,0:T(8,128)} async-done(((f32[768,1536]{1,0:T(8,128)}), f32[48,1536]{1,0:T(8,128)}) %reduce-scatter.27.cloned.1.call-update) | async-done | bytes 294928 | tf_op jit(solution)/shard_map/reduce_scatter | solution.py:295
  815.0 61.7 %reduce-scatter.25.cloned.1.call-done = f32[384,48]{0,1:T(8,128)} async-done(((f32[384,768]{0,1:T(8,128)}), f32[384,48]{0,1:T(8,128)}) %reduce-scatter.25.cloned.1.call-update) | async-done | bytes 73744 | tf_op jit(solution)/shard_map/reduce_scatter | solution.py:294
  876.7 61.2 %reduce-scatter.35.cloned.1.call-done = f32[48,384]{1,0:T(8,128)} async-done(((f32[768,384]{1,0:T(8,128)}), f32[48,384]{1,0:T(8,128)}) %reduce-scatter.35.cloned.1.call-update) | async-done | bytes 73744
  937.9 61.6 %reduce-scatter.31.cloned.1.call-done = f32[48,384]{1,0:T(8,128)} async-done(((f32[768,384]{1,0:T(8,128)}), f32[48,384]{1,0:T(8,128)}) %reduce-scatter.31.cloned.1.call-update) | async-done | bytes 73744
  999.5 61.4 %reduce-scatter.33.cloned.1.call-done = f32[48,384]{1,0:T(8,128)} async-done(((f32[768,384]{1,0:T(8,128)}), f32[48,384]{1,0:T(8,128)}) %reduce-scatter.33.cloned.1.call-update) | async-done | bytes 73744
  (262 shorter events, 222.7 us)
Async XLA Ops:
  8.1 57.5 %copy-start.23 = (bf16[384,48]{0,1:T(8,128)(2,1)S(1)}, bf16[384,48]{0,1:T(8,128)(2,1)}, u32[]{:S(2)}) copy-start(bf16[384,48]{0,1:T(8,128)(2,1)} %param.29) | copy-start | bytes 110596
  8.1 79.8 %all-gather.9.cloned.1.call-start = ((), (), s32[]{:S(2)}) async-start(), calls=%async_computation.10 | async-start | bytes 2359296 | tf_op jit(solution)/shard_map/all_gather | solution.py:175
  8.1 1.6 collective-permute-start
  10.6 5.5 collective-permute-start.1
  13.5 158.8 %reduce-scatter.17.cloned.1.call-start = ((), (), s32[]{:S(2)}) async-start(), calls=%async_computation.11 | async-start | bytes 4718592 | tf_op jit(solution)/shard_map/reduce_scatter | solution.py:196
  16.1 24.2 %collective-permute-start.2 = (bf16[4,48,384]{2,1,0:T(8,128)(2,1)S(1)}, bf16[4,48,384]{2,1,0:T(8,128)(2,1)S(1)}, u32[]{:S(2)}, u32[]{:S(2)}) collective-permute-start(bf16[4,48,384]{2,1,0:T(8,128)(2,1)S(1)} %bitcast.157), channel_id=1, source_target_pairs={{0,8},{2,10},{4,12},{6,14},{8,0},{10,2},{12,4},{14,6},{16,24},{18,... | collective-permute-start | bytes 442376 | tf_op jit(solution)/shard_map/ppermute | solution.py:26
  40.5 47.2 %collective-permute-start.3 = (bf16[8,48,384]{2,1,0:T(8,128)(2,1)S(1)}, bf16[8,48,384]{2,1,0:T(8,128)(2,1)S(1)}, u32[]{:S(2)}, u32[]{:S(2)}) collective-permute-start(bf16[8,48,384]{2,1,0:T(8,128)(2,1)S(1)} %bitcast.153), channel_id=1, source_target_pairs={{0,16},{2,18},{4,20},{6,22},{8,24},{10,26},{12,28},{14,30},{16,0},... | collective-permute-start | bytes 884744 | tf_op jit(solution)/shard_map/ppermute | solution.py:26
  131.4 44.8 %all-gather.13.cloned.1.call-start = ((), (), s32[]{:S(2)}) async-start(), calls=%async_computation.13 | async-start | bytes 2506752 | tf_op jit(solution)/shard_map/all_gather | solution.py:172
  132.0 70.7 %all-gather.11.cloned.1.call-start = ((), (), s32[]{:S(2)}) async-start(), calls=%async_computation.12 | async-start | bytes 2359296 | tf_op jit(solution)/shard_map/all_gather | solution.py:199
  175.5 71.9 %all-gather.15.cloned.1.call-start = ((), (), s32[]{:S(2)}) async-start(), calls=%async_computation.14 | async-start | bytes 2506752 | tf_op jit(solution)/shard_map/all_gather | solution.py:173
  176.1 120.1 %reduce-scatter.19.cloned.1.call-start = ((), (), s32[]{:S(2)}) async-start(), calls=%async_computation.15 | async-start | bytes 4718592 | tf_op jit(solution)/shard_map/reduce_scatter | solution.py:203
  254.3 77.1 %all-gather.17.cloned.1.call-start = ((), (), s32[]{:S(2)}) async-start(), calls=%async_computation.16 | async-start | bytes 2359296 | tf_op jit(solution)/shard_map/all_gather | solution.py:223
  304.3 72.1 %all-gather.19.cloned.1.call-start = ((), (), s32[]{:S(2)}) async-start(), calls=%async_computation.17 | async-start | bytes 2506752 | tf_op jit(solution)/shard_map/all_gather | solution.py:221
  305.0 114.7 %all-gather.21.cloned.1.call-start = ((), (), s32[]{:S(2)}) async-start(), calls=%async_computation.18 | async-start | bytes 2506752 | tf_op jit(solution)/shard_map/all_gather | solution.py:220
  305.8 162.8 %reduce-scatter.21.cloned.1.call-start = ((), (), s32[]{:S(2)}) async-start(), calls=%async_computation.19 | async-start | bytes 4718592 | tf_op jit(solution)/shard_map/reduce_scatter | solution.py:239
  426.6 134.8 %all-gather.23.cloned.1.call-start = ((), (), s32[]{:S(2)}) async-start(), calls=%async_computation.20 | async-start | bytes 2359296 | tf_op jit(solution)/shard_map/all_gather | solution.py:245
  472.6 68.5 %copy-start.27 = (bf16[48,384]{1,0:T(8,128)(2,1)S(1)}, bf16[48,384]{1,0:T(8,128)(2,1)}, u32[]{:S(2)}) copy-start(bf16[48,384]{1,0:T(8,128)(2,1)} %param.27) | copy-start | bytes 110596
  475.4 228.5 %reduce-scatter.23.cloned.1.call-start = ((), (), s32[]{:S(2)}) async-start(), calls=%async_computation.21 | async-start | bytes 2359296 | tf_op jit(solution)/shard_map/reduce_scatter | solution.py:287
  631.7 104.2 %reduce-scatter.29.cloned.1.call-start = ((), (), s32[]{:S(2)}) async-start(), calls=%async_computation.24 | async-start | bytes 5013504 | tf_op jit(solution)/shard_map/reduce_scatter | solution.py:296
  639.0 176.1 %reduce-scatter.27.cloned.1.call-start = ((), (), s32[]{:S(2)}) async-start(), calls=%async_computation.23 | async-start | bytes 5013504 | tf_op jit(solution)/shard_map/reduce_scatter | solution.py:295
  646.2 230.5 %reduce-scatter.25.cloned.1.call-start = ((), (), s32[]{:S(2)}) async-start(), calls=%async_computation.22 | async-start | bytes 1253376 | tf_op jit(solution)/shard_map/reduce_scatter | solution.py:294
  650.9 287.1 %reduce-scatter.35.cloned.1.call-start = ((), (), s32[]{:S(2)}) async-start(), calls=%async_computation.27 | async-start | bytes 1253376
  654.6 344.9 %reduce-scatter.31.cloned.1.call-start = ((), (), s32[]{:S(2)}) async-start(), calls=%async_computation.25 | async-start | bytes 1253376
  658.4 402.6 %reduce-scatter.33.cloned.1.call-start = ((), (), s32[]{:S(2)}) async-start(), calls=%async_computation.26 | async-start | bytes 1253376
  (47 other events, 718.9 us)
Sparse Core Ops, SparseCore 0:
  13.6 27.4 all-gather.8
  131.5 40.6 reduce-scatter.16
  254.4 41.7 reduce-scatter.18
  426.7 41.7 reduce-scatter.20
  475.5 27.1 all-gather.22
Sparse Core Ops, SparseCore 1:
  134.2 39.6 all-gather.12
  175.9 26.7 all-gather.10
  204.9 42.5 all-gather.14
  304.4 27.0 all-gather.16
  333.8 42.6 all-gather.18
  378.7 40.9 all-gather.20
  631.8 23.6 reduce-scatter.22
  659.8 76.1 reduce-scatter.28
  740.3 74.7 reduce-scatter.26
  819.2 57.4 reduce-scatter.24
  880.8 57.1 reduce-scatter.34
  942.1 57.3 reduce-scatter.30
  1003.6 57.3 reduce-scatter.32
